TPU v7x, 32 devices: a whole 2x2x4 slice. The times are simulated.
32 devices in a mesh: stream: 2 (over core), dp: 16 (over z, y, x).
Axes of the slice: x: 2, y: 2, z: 4, core: 2. Of those that a mesh axis runs over, the one named last changes fastest.
Arguments:
- layer_input: bfloat16 [2, 16384, 768], P('stream', 'dp'), may hold values from -6 to 6
- pair_group: int32 [256], P('dp'), may hold values from 0 to 108, as said below
- query_weight: bfloat16 [768, 768], replicated, may hold values from -0.21875 to 0.21875
- query_bias: float32 [768], replicated, may hold values from -4 to 4
- key_weight: bfloat16 [768, 768], replicated, may hold values from -0.21875 to 0.21875
- value_weight: bfloat16 [768, 768], replicated, may hold values from -0.21875 to 0.21875
- value_bias: float32 [768], replicated, may hold values from -4 to 4
- out_weight: bfloat16 [768, 768], replicated, may hold values from -1 to 1
- out_bias: float32 [768], replicated, may hold values from -4 to 4
- mixer_gain: float32 [768], replicated, may hold values from 0.1 to 1.9
- mixer_shift: float32 [768], replicated, may hold values from -4 to 4
- up_weight: bfloat16 [768, 3072], replicated, may hold values from -0.21875 to 0.21875
- up_bias: float32 [3072], replicated, may hold values from -4 to 4
- down_weight: bfloat16 [3072, 768], replicated, may hold values from -0.109375 to 0.109375
- down_bias: float32 [768], replicated, may hold values from -4 to 4
- final_gain: float32 [768], replicated, may hold values from 0.1 to 1.9
- final_shift: float32 [768], replicated, may hold values from -4 to 4
- upstream: bfloat16 [2, 16384, 768], P('stream', 'dp'), may hold values from -0.75 to 0.75
Outputs:
- layer_output: bfloat16 [2, 16384, 768], P('stream', 'dp')
- input_grad: float32 [2, 16384, 768], P('stream', 'dp')
- total_loss: float32 [2, 256], P('stream', 'dp')
- query_weight_grad: float32 [768, 768], replicated
- query_bias_grad: float32 [768], replicated
- key_weight_grad: float32 [768, 768], replicated
- value_weight_grad: float32 [768, 768], replicated
- value_bias_grad: float32 [768], replicated
- out_weight_grad: float32 [768, 768], replicated
- out_bias_grad: float32 [768], replicated
- mixer_gain_grad: float32 [768], replicated
- mixer_shift_grad: float32 [768], replicated
- up_weight_grad: float32 [768, 3072], replicated
- up_bias_grad: float32 [3072], replicated
- down_weight_grad: float32 [3072, 768], replicated
- down_bias_grad: float32 [768], replicated
- final_gain_grad: float32 [768], replicated
- final_shift_grad: float32 [768], replicated
Inputs may be any that keep to these rules, and one draw needn't show every extreme that they name: `pair_group`: every one of the 109 ids names 2 or more pairs; the first and the last pair have the same id.
All inputs are finite; a program needn't handle non-finite values.
Results may differ from a plain program's by a relative error of at most 0.014.
Values may be sent and summed in bfloat16 or wider, within the bound.
No kernel may reach another device: no remote copies, remote signals or barrier semaphores. Data moves between devices by JAX's collectives and lax.ppermute only.
A program may use at most 256 MiB of HBM per device.

v0:
```python
import math
import jax
import jax.numpy as jnp
from jax import lax
from jax.sharding import PartitionSpec as P

D = 768
HEADS = 12
HD = 64
GROUPS = 109
MARGIN = 0.3
LOGIT_SCALE = 30.0
NORM_EPS = 1e-12
UNIT_EPS = 1e-06
highest = lax.Precision.HIGHEST


def norm_forward(values, gain, shift):
    centred = values - jnp.mean(values, axis=-1, keepdims=True)
    inv_std = lax.rsqrt(jnp.mean(centred * centred, axis=-1, keepdims=True) + NORM_EPS)
    normed_hat = centred * inv_std
    return (normed_hat * gain + shift, normed_hat, inv_std)


def norm_backward(grad_out, normed_hat, inv_std, gain):
    grad_hat = grad_out * gain
    mean_grad = jnp.mean(grad_hat, axis=-1, keepdims=True)
    mean_cross = jnp.mean(grad_hat * normed_hat, axis=-1, keepdims=True)
    grad_in = inv_std * (grad_hat - mean_grad - normed_hat * mean_cross)
    return (grad_in, jnp.sum(grad_out * normed_hat, axis=0), jnp.sum(grad_out, axis=0))


def gelu_slope(values):
    normal_cdf = 0.5 * (1.0 + lax.erf(values * (1.0 / math.sqrt(2.0))))
    return normal_cdf + values * jnp.exp(-0.5 * values * values) * (1.0 / math.sqrt(2.0 * math.pi))


def to_heads(matrix, key_span):
    return matrix.reshape(-1, key_span, HEADS, HD)


def attend_scores(query_heads, key_heads, key_mask, factor):
    raw_scores = (
        jnp.einsum("bqhd,bkhd->bhqk", query_heads, key_heads, preferred_element_type=jnp.float32)
        * factor
    )
    return jnp.where(key_mask, raw_scores, -jnp.inf)


def outer_sum(left, right):
    return jnp.einsum("ri,rj->ij", left, right, preferred_element_type=jnp.float32)


def back_project(grad_rows, weight):
    return jnp.einsum("re,de->rd", grad_rows, weight, preferred_element_type=jnp.float32)


def shards(
    layer_input,
    pair_group,
    query_weight,
    query_bias,
    key_weight,
    value_weight,
    value_bias,
    out_weight,
    out_bias,
    mixer_gain,
    mixer_shift,
    up_weight,
    up_bias,
    down_weight,
    down_bias,
    final_gain,
    final_shift,
    upstream,
):
    tokens = layer_input[0]
    token_count = tokens.shape[0]
    seq_count = pair_group.shape[0]
    seq_len = token_count // seq_count
    key_span = 2 * seq_len
    factor = 1.0 / math.sqrt(HD)
    place = jnp.arange(key_span) // seq_len
    key_mask = place[:, None] == place[None, :]
    queries = (
        jnp.dot(tokens, query_weight, preferred_element_type=jnp.float32) + query_bias
    ).astype(jnp.bfloat16)
    keys_all = jnp.dot(tokens, key_weight, preferred_element_type=jnp.float32).astype(jnp.bfloat16)
    values_all = (
        jnp.dot(tokens, value_weight, preferred_element_type=jnp.float32) + value_bias
    ).astype(jnp.bfloat16)
    query_heads = to_heads(queries, key_span)
    key_heads = to_heads(keys_all, key_span)
    value_heads = to_heads(values_all, key_span)
    scores = attend_scores(query_heads, key_heads, key_mask, factor)
    row_top = jnp.max(scores, axis=-1, keepdims=True)
    log_total = row_top + jnp.log(jnp.sum(jnp.exp(scores - row_top), axis=-1, keepdims=True))
    probs_low = jnp.exp(scores - log_total).astype(jnp.bfloat16)
    context = jnp.einsum(
        "bhqk,bkhd->bqhd", probs_low, value_heads, preferred_element_type=jnp.float32
    )
    context = context.astype(jnp.bfloat16).reshape(token_count, D)
    attended = jnp.dot(context, out_weight, preferred_element_type=jnp.float32) + out_bias
    normed, hat_one, inv_one = norm_forward(
        tokens.astype(jnp.float32) + attended, mixer_gain, mixer_shift
    )
    normed_low = normed.astype(jnp.bfloat16)
    hidden_pre = jnp.dot(normed_low, up_weight, preferred_element_type=jnp.float32) + up_bias
    activated = jax.nn.gelu(hidden_pre, approximate=False).astype(jnp.bfloat16)
    branch = jnp.dot(activated, down_weight, preferred_element_type=jnp.float32) + down_bias
    final_rows, hat_two, inv_two = norm_forward(normed + branch, final_gain, final_shift)
    layer_output = final_rows.astype(jnp.bfloat16)[None]
    lead_rows = final_rows.reshape(seq_count, seq_len, D)[:, 0, :]
    lead_inv = lax.rsqrt(jnp.sum(lead_rows * lead_rows, axis=-1, keepdims=True) + UNIT_EPS)
    unit_rows = (lead_rows * lead_inv).astype(jnp.bfloat16)
    pairs_all = seq_count * lax.axis_size("dp")
    all_groups = lax.all_gather(pair_group, "dp", axis=0, tiled=True)
    everyone = lax.all_gather(unit_rows, ("stream", "dp"), axis=0, tiled=True).reshape(
        2, pairs_all, D
    )
    half_index = lax.axis_index("stream")
    offset = lax.axis_index("dp") * seq_count
    others = lax.dynamic_index_in_dim(everyone, 1 - half_index, 0, keepdims=False)
    group_range = jnp.arange(GROUPS, dtype=jnp.int32)
    own_hits = (pair_group[:, None] == group_range[None, :]).astype(jnp.float32)
    counts = lax.psum(jnp.sum(own_hits, axis=0), "dp")
    row_weight = pairs_all / GROUPS / jnp.sum(own_hits * counts[None, :], axis=1)
    sim_scores = LOGIT_SCALE * jnp.einsum(
        "id,jd->ij", unit_rows, others, preferred_element_type=jnp.float32
    )
    columns = jnp.arange(pairs_all, dtype=jnp.int32)
    diagonal = columns[None, :] == (offset + jnp.arange(seq_count, dtype=jnp.int32))[:, None]
    same_group = pair_group[:, None] == all_groups[None, :]
    logits = sim_scores - LOGIT_SCALE * MARGIN * diagonal.astype(jnp.float32)
    masked = jnp.where(same_group, logits, -jnp.inf)
    loss_top = jnp.max(masked, axis=1, keepdims=True)
    exp_terms = jnp.exp(masked - loss_top)
    row_sums = jnp.sum(exp_terms, axis=1, keepdims=True)
    own_logit = jnp.sum(jnp.where(diagonal, logits, 0.0), axis=1)
    row_loss = loss_top[:, 0] + jnp.log(row_sums[:, 0]) - own_logit
    loss_rows = (row_weight * row_loss)[None]
    dlogits = row_weight[:, None] * (exp_terms / row_sums - diagonal.astype(jnp.float32))
    grad_own = LOGIT_SCALE * jnp.dot(dlogits, others.astype(jnp.float32), precision=highest)
    grad_cols = LOGIT_SCALE * jnp.dot(dlogits.T, unit_rows.astype(jnp.float32), precision=highest)
    grad_terms = jnp.zeros((2, pairs_all, D), jnp.float32)
    grad_terms = lax.dynamic_update_slice(grad_terms, grad_cols[None], (1 - half_index, 0, 0))
    grad_terms = lax.dynamic_update_slice(grad_terms, grad_own[None], (half_index, offset, 0))
    unit_grad = lax.psum_scatter(
        grad_terms.reshape(2 * pairs_all, D), ("stream", "dp"), scatter_dimension=0, tiled=True
    )
    cross = jnp.sum(lead_rows * unit_grad, axis=-1, keepdims=True)
    lead_grad = lead_inv * unit_grad - lead_inv * lead_inv * lead_inv * cross * lead_rows
    final_grad = upstream[0].astype(jnp.float32).reshape(seq_count, seq_len, D)
    final_grad = final_grad.at[:, 0, :].add(lead_grad).reshape(token_count, D)
    dresid_two, final_gain_grad, final_shift_grad = norm_backward(
        final_grad, hat_two, inv_two, final_gain
    )
    dbranch = dresid_two.astype(jnp.bfloat16)
    down_weight_grad = outer_sum(activated, dbranch)
    down_bias_grad = jnp.sum(dbranch, axis=0, dtype=jnp.float32)
    dpre = (back_project(dbranch, down_weight) * gelu_slope(hidden_pre)).astype(jnp.bfloat16)
    up_weight_grad = outer_sum(normed_low, dpre)
    up_bias_grad = jnp.sum(dpre, axis=0, dtype=jnp.float32)
    dnormed = dresid_two + back_project(dpre, up_weight)
    dresid_one, mixer_gain_grad, mixer_shift_grad = norm_backward(
        dnormed, hat_one, inv_one, mixer_gain
    )
    datt = dresid_one.astype(jnp.bfloat16)
    out_weight_grad = outer_sum(context, datt)
    out_bias_grad = jnp.sum(datt, axis=0, dtype=jnp.float32)
    dcontext = back_project(datt, out_weight).astype(jnp.bfloat16)
    dcontext_heads = to_heads(dcontext, key_span)
    again = attend_scores(query_heads, key_heads, key_mask, factor)
    probs_f = jnp.exp(again - log_total)
    dprobs = jnp.einsum(
        "bqhd,bkhd->bhqk", dcontext_heads, value_heads, preferred_element_type=jnp.float32
    )
    row_dot = jnp.sum(probs_f * dprobs, axis=-1, keepdims=True)
    dscores = (probs_f * (dprobs - row_dot)).astype(jnp.bfloat16)
    dqueries = (
        jnp.einsum("bhqk,bkhd->bqhd", dscores, key_heads, preferred_element_type=jnp.float32)
        * factor
    )
    dqueries = dqueries.astype(jnp.bfloat16).reshape(token_count, D)
    dkeys = (
        jnp.einsum("bhqk,bqhd->bkhd", dscores, query_heads, preferred_element_type=jnp.float32)
        * factor
    )
    dkeys = dkeys.astype(jnp.bfloat16).reshape(token_count, D)
    dvalues = (
        jnp.einsum(
            "bhqk,bqhd->bkhd",
            probs_f.astype(jnp.bfloat16),
            dcontext_heads,
            preferred_element_type=jnp.float32,
        )
        .astype(jnp.bfloat16)
        .reshape(token_count, D)
    )
    query_weight_grad = outer_sum(tokens, dqueries)
    query_bias_grad = jnp.sum(dqueries, axis=0, dtype=jnp.float32)
    key_weight_grad = outer_sum(tokens, dkeys)
    value_weight_grad = outer_sum(tokens, dvalues)
    value_bias_grad = jnp.sum(dvalues, axis=0, dtype=jnp.float32)
    input_grad = (
        dresid_one
        + back_project(dqueries, query_weight)
        + back_project(dkeys, key_weight)
        + back_project(dvalues, value_weight)
    )
    local_grads = [
        query_weight_grad,
        query_bias_grad,
        key_weight_grad,
        value_weight_grad,
        value_bias_grad,
        out_weight_grad,
        out_bias_grad,
        mixer_gain_grad,
        mixer_shift_grad,
        up_weight_grad,
        up_bias_grad,
        down_weight_grad,
        down_bias_grad,
        final_gain_grad,
        final_shift_grad,
    ]
    flat_grads = jnp.concatenate([piece.reshape(-1) for piece in local_grads])
    total_len = flat_grads.shape[0]
    share_devices = lax.axis_size(("stream", "dp"))
    share_count = -(-total_len // share_devices)
    share_width = -(-share_count // 128) * 128
    flat_grads = flat_grads.reshape(share_devices, share_count)
    flat_grads = jnp.pad(flat_grads, ((0, 0), (0, share_width - share_count))).reshape(-1, 128)
    shares = lax.psum_scatter(flat_grads, ("stream", "dp"), scatter_dimension=0, tiled=True)
    reduced = lax.all_gather(
        shares.astype(jnp.bfloat16), ("stream", "dp"), axis=0, tiled=True
    ).astype(shares.dtype)
    reduced = reduced.reshape(share_devices, share_width)[:, :share_count].reshape(-1)
    summed = []
    cursor = 0
    for piece in local_grads:
        piece_len = piece.size
        summed.append(reduced[cursor : cursor + piece_len].reshape(piece.shape))
        cursor = cursor + piece_len
    return (
        layer_output,
        input_grad[None],
        loss_rows,
        summed[0],
        summed[1],
        summed[2],
        summed[3],
        summed[4],
        summed[5],
        summed[6],
        summed[7],
        summed[8],
        summed[9],
        summed[10],
        summed[11],
        summed[12],
        summed[13],
        summed[14],
    )


def solution(mesh):
    return jax.shard_map(
        shards,
        mesh=mesh,
        in_specs=(
            P("stream", "dp", None),
            P("dp"),
            P(),
            P(),
            P(),
            P(),
            P(),
            P(),
            P(),
            P(),
            P(),
            P(),
            P(),
            P(),
            P(),
            P(),
            P(),
            P("stream", "dp", None),
        ),
        out_specs=(
            P("stream", "dp", None),
            P("stream", "dp", None),
            P("stream", "dp"),
            P(),
            P(),
            P(),
            P(),
            P(),
            P(),
            P(),
            P(),
            P(),
            P(),
            P(),
            P(),
            P(),
            P(),
            P(),
        ),
        check_vma=False,
    )
```

profile of v0, /device:TPU:0, one launch (start us, length us, event | category | flops | bytes accessed | tf_op | source)
XLA Modules:
  0.0 1631.6 jit_solution(9747999156966175325)
XLA Ops:
  8.5 43.5 %psum.7 = f32[109]{0:T(128)S(1)} all-reduce(f32[109]{0:T(128)S(1)} %convert_reduce_fusion.5), channel_id=1, replica_groups=mesh['stream'=2,'dp'=16] {'dp'}, use_global_device_ids=true, to_apply=%region_8.9 | all-reduce | flops 109 | bytes 872 | tf_op jit(solution)/shard_map/psum | solution.py:127
  56.1 9.0 all-reduce.1
  97.9 34.5 %fusion.3 = (bf16[1024,3072]{1,0:T(8,128)(2,1)S(1)}, f32[1024,3072]{1,0:T(8,128)}) fusion(f32[3072]{0:T(1024)S(1)} %copy-done.61, bf16[768,3072]{1,0:T(8,128)(2,1)S(1)} %bitcast.204, f32[1024,768]{1,0:T(8,128)S(1)} %get-tuple-element.63, f32[768]{0:T(1024)S(1)} %copy-done.37, f32[768]{0:T(1024)S(1)} %copy-done.32, f32[1024]{0:T(1024)S(1)} %add_rsqrt_fusion.1, ...), kind=kOutput, calls=%fused_computation.6 | convolution fusion | flops 5043388416 | bytes 26765312 | tf_op jit(solution)/shard_map/dot_general | solution.py:109
  132.5 5.5 fusion.100
  141.3 69.7 %all_gather.10 = bf16[512,768]{1,0:T(8,128)(2,1)S(1)} all-gather(bf16[16,768]{1,0:T(8,128)(2,1)S(1)} %fusion.71), channel_id=1, replica_groups=mesh['stream'=2,'dp'=16] {'stream','dp'}, dimensions={0}, use_global_device_ids=true | all-gather | bytes 811008 | tf_op jit(solution)/shard_map/all_gather | solution.py:119
  219.3 93.5 %reduce-scatter.4.cloned.1.call-done = f32[16,768]{1,0:T(8,128)} async-done(((f32[512,768]{1,0:T(8,128)}), f32[16,768]{1,0:T(8,128)}) %reduce-scatter.4.cloned.1.call-update) | async-done | bytes 49168 | tf_op jit(solution)/shard_map/reduce_scatter | solution.py:149
  327.6 10.3 fusion.86
  337.9 12.5 convert_reduce_fusion
  350.4 6.5 multiply_reduce_fusion.1
  356.9 8.9 convolution_bitcast_fusion
  375.1 6.4 convert_reduce_fusion.3
  386.1 4.9 fusion.41
  393.1 10.8 reshape.345
  404.0 9.6 copy.134
  460.2 21.3 %dynamic-update-slice.6 = f32[7087104]{0:T(1024)} dynamic-update-slice(f32[7087104]{0:T(1024)} %constant_dynamic-update-slice_fusion.8, f32[589824]{0:T(1024)} %reshape.341, s32[]{} %constant.180) | dynamic-update-slice | bytes 4718596
  481.5 21.2 %dynamic-update-slice.7 = f32[7087104]{0:T(1024)} dynamic-update-slice(f32[7087104]{0:T(1024)} %dynamic-update-slice.6, f32[589824]{0:T(1024)} %reshape.342, s32[]{} %constant.181) | dynamic-update-slice | bytes 4718596
  504.0 20.3 %dynamic-update-slice.9 = f32[7087104]{0:T(1024)} dynamic-update-slice(f32[7087104]{0:T(1024)} %constant_dynamic-update-slice_fusion.7, f32[589824]{0:T(1024)S(1)} %reshape.343, s32[]{} %constant.183) | dynamic-update-slice | bytes 4718596
  528.2 80.3 %dynamic-update-slice.13 = f32[7087104]{0:T(1024)} dynamic-update-slice(f32[7087104]{0:T(1024)} %constant_dynamic-update-slice_fusion.4, f32[2359296]{0:T(1024)} %bitcast.172, s32[]{} %constant.187) | dynamic-update-slice | bytes 18874372
  609.9 80.8 %dynamic-update-slice.15 = f32[7087104]{0:T(1024)} dynamic-update-slice(f32[7087104]{0:T(1024)} %constant_dynamic-update-slice_fusion.3, f32[2359296]{0:T(1024)} %reshape.345, s32[]{} %constant.189) | dynamic-update-slice | bytes 18874372
  694.5 37.8 %reshape.346 = f32[32,221472]{1,0:T(8,128)} reshape(f32[7087104]{0:T(1024)} %constant_dynamic-update-slice_fusion) | data formatting | bytes 56696832 | tf_op jit(solution)/shard_map/reshape | solution.py:234
  732.3 20.9 %pad.6 = f32[32,221568]{1,0:T(8,128)} pad(f32[32,221472]{1,0:T(8,128)} %reshape.346, f32[]{:T(128)} %constant.120.clone.1), padding=0_0x0_96 | pad | bytes 56709124 | tf_op jit(solution)/shard_map/jit(_pad)/pad | solution.py:235
  753.2 25.4 %reshape.347 = f32[55392,128]{1,0:T(8,128)} reshape(f32[32,221568]{1,0:T(8,128)} %pad.6) | data formatting | bytes 56721408 | tf_op jit(solution)/shard_map/reshape | solution.py:235
  778.7 605.0 %fusion = f32[1744,128]{1,0:T(8,128)S(1)} fusion(f32[55392,128]{1,0:T(8,128)} %reshape.347), kind=kCustom, calls=%all-reduce-scatter | all-reduce-scatter fusion | flops 7143425 | bytes 29253632
  1399.4 96.9 %all-gather.3.cloned.1.call-done = bf16[32,1731,128]{2,1,0:T(8,128)(2,1)} async-done(((bf16[1,1731,128]{2,1,0:T(8,128)(2,1)}), bf16[32,1731,128]{2,1,0:T(8,128)(2,1)}) %all-gather.3.cloned.1.call-update) | async-done | bytes 14180368 | tf_op jit(solution)/shard_map/all_gather | solution.py:237
  1496.2 12.8 copy.209
  1509.0 9.7 slice_convert_fusion
  1518.8 36.5 %reshape.361 = f32[7087104]{0:T(1024)} reshape(f32[32,221472]{1,0:T(8,128)} %slice_convert_fusion) | data formatting | bytes 56696832
  1558.0 8.3 slice.115
  1566.3 31.3 %slice.87 = f32[9228,768]{1,0:T(8,128)} reshape(f32[7087104]{0:T(1024)} %reshape.361) | data formatting | bytes 56696832 | tf_op jit(solution)/shard_map/slice | solution.py:245
  1597.6 8.1 slice.117
  1605.7 7.7 fusion.97
  1613.3 11.0 reshape.350
  (259 shorter events, 154.5 us)
Async XLA Ops:
  7.2 86.2 %copy-start = (bf16[768,768]{1,0:T(8,128)(2,1)S(1)}, bf16[768,768]{1,0:T(8,128)(2,1)}, u32[]{:S(2)}) copy-start(bf16[768,768]{1,0:T(8,128)(2,1)} %param.27) | copy-start | bytes 3538948
  7.2 305.6 %reduce-scatter.4.cloned.1.call-start = ((), (), s32[]{:S(2)}) async-start(), calls=%async_computation.1 | async-start | bytes 1622016 | tf_op jit(solution)/shard_map/reduce_scatter | solution.py:149
  65.2 24.6 %copy-start.29 = (pred[128,128]{0,1:T(8,128)(4,1)}, pred[128,128]{0,1:T(8,128)(4,1)S(1)}, u32[]{:S(2)}) copy-start(pred[128,128]{0,1:T(8,128)(4,1)S(1)} %broadcast_compare_fusion) | copy-start | bytes 49156
  93.5 39.0 %slice-start.2 = ((s8[4718592]{0:T(1024)(128)(4,1)}), s8[4194304]{0:T(1024)(128)(4,1)S(1)}, s32[]{:S(2)}) async-start(s8[4718592]{0:T(1024)(128)(4,1)} %bitcast.199), calls=%async_computation.5 | async-start | bytes 8388608
  95.2 37.2 %copy-start.5 = (f32[1024,768]{1,0:T(8,128)}, f32[1024,768]{1,0:T(8,128)S(1)}, u32[]{:S(2)}) copy-start(f32[1024,768]{1,0:T(8,128)S(1)} %get-tuple-element.63) | copy-start | bytes 9437188
  97.9 34.6 %slice-start.3 = ((s8[4718592]{0:T(1024)(128)(4,1)}), s8[524288]{0:T(1024)(128)(4,1)S(1)}, s32[]{:S(2)}) async-start(s8[4718592]{0:T(1024)(128)(4,1)} %bitcast.199), calls=%async_computation.6 | async-start | bytes 1048576
  97.9 34.6 %copy-start.65 = (f32[768]{0:T(1024)S(1)}, f32[768]{0:T(1024)}, u32[]{:S(2)}) copy-start(f32[768]{0:T(1024)} %param.34) | copy-start | bytes 9220
  138.7 72.3 %copy-start.39 = (s32[256]{0:T(256)S(1)}, s32[256]{0:T(256)}, u32[]{:S(2)}) copy-start(s32[256]{0:T(256)} %all-reduce.1) | copy-start | bytes 3076
  138.7 72.3 %copy-start.44 = (s32[16]{0:T(128)S(1)}, s32[16]{0:T(128)}, u32[]{:S(2)}) copy-start(s32[16]{0:T(128)} %param.21) | copy-start | bytes 196
  138.7 72.3 %copy-start.45 = (s32[16]{0:T(128)S(1)}, s32[16]{0:T(128)}, u32[]{:S(2)}) copy-start(s32[16]{0:T(128)} %iota_add_fusion) | copy-start | bytes 196
  138.7 72.8 %copy-start.53 = (f32[16]{0:T(128)S(1)}, f32[16]{0:T(128)}, u32[]{:S(2)}) copy-start(f32[16]{0:T(128)} %select_reduce_fusion.1) | copy-start | bytes 196
  140.5 71.6 %copy-start.18 = (f32[16,1,768]{2,1,0:T(1,128)}, f32[16,1,768]{2,1,0:T(1,128)S(1)}, u32[]{:S(2)}) copy-start(f32[16,1,768]{2,1,0:T(1,128)S(1)} %slice.104) | copy-start | bytes 147460
  141.2 70.9 %copy-start.46 = (f32[16]{0:T(128)}, f32[16]{0:T(128)S(1)}, u32[]{:S(2)}) copy-start(f32[16]{0:T(128)S(1)} %add_rsqrt_fusion.2) | copy-start | bytes 196
  141.3 70.8 %copy-start.31 = (bf16[16,768]{1,0:T(8,128)(2,1)}, bf16[16,768]{1,0:T(8,128)(2,1)S(1)}, u32[]{:S(2)}) copy-start(bf16[16,768]{1,0:T(8,128)(2,1)S(1)} %fusion.71) | copy-start | bytes 73732
  214.7 98.1 %copy-start.19 = (f32[16,1,768]{2,1,0:T(1,128)S(1)}, f32[16,1,768]{2,1,0:T(1,128)}, u32[]{:S(2)}) copy-start(f32[16,1,768]{2,1,0:T(1,128)} %copy-done.18) | copy-start | bytes 147460
  214.7 99.1 %copy-start.52 = (f32[16]{0:T(128)S(1)}, f32[16]{0:T(128)}, u32[]{:S(2)}) copy-start(f32[16]{0:T(128)} %copy-done.51) | copy-start | bytes 196
  214.7 99.1 %copy-start.47 = (f32[16]{0:T(128)S(1)}, f32[16]{0:T(128)}, u32[]{:S(2)}) copy-start(f32[16]{0:T(128)} %copy-done.46) | copy-start | bytes 196
  214.7 103.2 %copy-start.34 = (f32[768]{0:T(1024)S(1)}, f32[768]{0:T(1024)}, u32[]{:S(2)}) copy-start(f32[768]{0:T(1024)} %param.35) | copy-start | bytes 9220
  214.7 103.2 %copy-start.36 = (f32[1024]{0:T(1024)S(1)}, f32[1024]{0:T(1024)}, u32[]{:S(2)}) copy-start(f32[1024]{0:T(1024)} %copy-done.35) | copy-start | bytes 12292
  215.8 1280.4 %all-gather.3.cloned.1.call-start = ((), (), s32[]{:S(2)}) async-start(), calls=%async_computation.2 | async-start | bytes 14665728 | tf_op jit(solution)/shard_map/all_gather | solution.py:237
  323.4 14.4 slice-start.4
  327.5 22.8 %slice-start.8 = ((s8[4718592]{0:T(1024)(128)(4,1)}), s8[4194304]{0:T(1024)(128)(4,1)S(1)}, s32[]{:S(2)}) async-start(s8[4718592]{0:T(1024)(128)(4,1)} %bitcast.205), calls=%async_computation.11 | async-start | bytes 8388608
  337.9 12.5 copy-start.6
  337.9 12.5 slice-start.9
  502.7 22.9 %copy-start.50 = (f32[768]{0:T(1024)S(1)}, f32[768]{0:T(1024)}, u32[]{:S(2)}) copy-start(f32[768]{0:T(1024)} %get-tuple-element.32) | copy-start | bytes 9220
  502.7 24.2 %copy-start.49 = (f32[768]{0:T(1024)S(1)}, f32[768]{0:T(1024)}, u32[]{:S(2)}) copy-start(f32[768]{0:T(1024)} %get-tuple-element.37) | copy-start | bytes 9220
  528.2 80.3 %copy-start.43 = (f32[3072]{0:T(1024)S(1)}, f32[3072]{0:T(1024)}, u32[]{:S(2)}) copy-start(f32[3072]{0:T(1024)} %get-tuple-element.77) | copy-start | bytes 36868
  609.9 80.8 %copy-start.41 = (f32[768]{0:T(1024)S(1)}, f32[768]{0:T(1024)}, u32[]{:S(2)}) copy-start(f32[768]{0:T(1024)} %get-tuple-element.40) | copy-start | bytes 9220
  609.9 82.1 %copy-start.42 = (f32[768]{0:T(1024)S(1)}, f32[768]{0:T(1024)}, u32[]{:S(2)}) copy-start(f32[768]{0:T(1024)} %get-tuple-element.30) | copy-start | bytes 9220
  609.9 83.4 %copy-start.40 = (f32[768]{0:T(1024)S(1)}, f32[768]{0:T(1024)}, u32[]{:S(2)}) copy-start(f32[768]{0:T(1024)} %get-tuple-element.35) | copy-start | bytes 9220
  778.7 611.8 %copy-start.24 = (bf16[8,128,12,64]{1,0,3,2:T(8,128)(2,1)S(1)}, bf16[8,128,12,64]{1,0,3,2:T(8,128)(2,1)}, u32[]{:S(2)}) copy-start(bf16[8,128,12,64]{1,0,3,2:T(8,128)(2,1)} %copy-done.23) | copy-start | bytes 4718596
  1383.7 4.4 collective-permute-start
  (48 other events, 168.0 us)
Sparse Core Ops, SparseCore 0:
  215.9 96.8 reduce-scatter.3
  1390.6 105.6 all-gather.2
where the time goes:
time: 1650 us; the launch traced here: 1630 us
  blocking collectives  727 us (44%)
  local copies, waits for them, and re-layouts  523 us (32%)
  waiting for transfers between devices  194 us (12%)
  matrix products  133 us (8%)
  other arithmetic  37.2 us (2%)
    unnamed x2, blocking collectives  614 us
    unnamed x181, local copies, waits for them, and re-layouts  317 us
    all_gather x1, waiting for transfers between devices, shards(): lax.all_gather(shares.astype(jnp.bfloat16), ('stream', 'dp'), axis=0, til...  96.9 us
    reduce_scatter x1, waiting for transfers between devices, shards(): lax.psum_scatter(grad_terms.reshape(2 * pairs_all, D), ('stream', 'dp'),...  93.5 us
    all_gather x1, blocking collectives, shards(): lax.all_gather(unit_rows, ('stream', 'dp'), axis=0, tiled=True)  69.7 us
    slice x6, local copies, waits for them, and re-layouts, shards(): summed.append(reduced[cursor:cursor + piece_len].reshape(piece.shape))  58 us
    psum x1, blocking collectives, shards(): counts = lax.psum(jnp.sum(own_hits, axis=0), 'dp')  43.5 us
    reshape x1, local copies, waits for them, and re-layouts, shards(): flat_grads = flat_grads.reshape(share_devices, share_count)  37.8 us
  transfers between devices with their start and end apart: 3, of which 3 were waited for; matrix products, arithmetic and copies ran while one was open for 1% of the time, Pallas kernels for 0%

commit v1 on v0

--- a/solution.py
+++ b/solution.py
@@ -75,6 +75,12 @@
     final_shift,
     upstream,
 ):
+
+    def play_pipes(body):
+        side_arr = jax.lax.all_gather(body, "dp")
+        q_next = jnp.sum(side_arr, 0)
+        return q_next
+
     tokens = layer_input[0]
     token_count = tokens.shape[0]
     seq_count = pair_group.shape[0]
@@ -124,7 +130,7 @@
     others = lax.dynamic_index_in_dim(everyone, 1 - half_index, 0, keepdims=False)
     group_range = jnp.arange(GROUPS, dtype=jnp.int32)
     own_hits = (pair_group[:, None] == group_range[None, :]).astype(jnp.float32)
-    counts = lax.psum(jnp.sum(own_hits, axis=0), "dp")
+    counts = play_pipes(jnp.sum(own_hits, axis=0))
     row_weight = pairs_all / GROUPS / jnp.sum(own_hits * counts[None, :], axis=1)
     sim_scores = LOGIT_SCALE * jnp.einsum(
         "id,jd->ij", unit_rows, others, preferred_element_type=jnp.float32

time: 1650 us -> 1650 us (level)
    unnamed x2 -> x3, blocking collectives: 614 us -> 660 us
    psum x1 -> x0, blocking collectives: 43.5 us -> none  [shards(): counts = lax.psum(jnp.sum(own_hits, axis=0), 'dp')]
    unnamed x181 -> x183, local copies, waits for them, and re-layouts: 317 us -> 317 us
where the time goes in v1:
time: 1650 us; the launch traced here: 1630 us
  blocking collectives  728 us (44%)
  local copies, waits for them, and re-layouts  524 us (32%)
  waiting for transfers between devices  191 us (12%)
  matrix products  133 us (8%)
  other arithmetic  37.2 us (2%)
  between operations  16.7 us (1%)
    unnamed x3, blocking collectives  660 us
    unnamed x183, local copies, waits for them, and re-layouts  317 us
    all_gather x1, waiting for transfers between devices, shards(): lax.all_gather(shares.astype(jnp.bfloat16), ('stream', 'dp'), axis=0, til...  96.8 us
    reduce_scatter x1, waiting for transfers between devices, shards(): lax.psum_scatter(grad_terms.reshape(2 * pairs_all, D), ('stream', 'dp'),...  91.3 us
    all_gather x1, blocking collectives, shards(): lax.all_gather(unit_rows, ('stream', 'dp'), axis=0, tiled=True)  68 us
    slice x6, local copies, waits for them, and re-layouts, shards(): summed.append(reduced[cursor:cursor + piece_len].reshape(piece.shape))  58 us
    reshape x1, local copies, waits for them, and re-layouts, shards(): flat_grads = flat_grads.reshape(share_devices, share_count)  37.8 us
    dot_general x1, matrix products, shards(): jnp.dot(normed_low, up_weight, preferred_element_type=jnp.float32) + up_bias  34.5 us
  transfers between devices with their start and end apart: 3, of which 3 were waited for; matrix products, arithmetic and copies ran while one was open for 1% of the time, Pallas kernels for 0%

profile of v1, /device:TPU:0, one launch (start us, length us, event | category | flops | bytes accessed | tf_op | source)
XLA Modules:
  0.0 1631.4 jit_solution(14366901326113563180)
XLA Ops:
  11.9 16.7 %all-reduce.2 = s32[256]{0:T(256)} all-reduce(s32[256]{0:T(256)S(1)} %dynamic-update-slice.4), channel_id=1, replica_groups=mesh['stream'=2,'dp'=16] {'dp'}, use_global_device_ids=true, to_apply=%add.2 | all-reduce | flops 256 | bytes 2048
  28.8 38.6 %all-reduce.1 = f32[1744]{0:T(1024)S(1)} all-reduce(f32[1744]{0:T(1024)S(1)} %dynamic-update-slice.3), channel_id=2, replica_groups=mesh['stream'=2,'dp'=16] {'dp'}, use_global_device_ids=true, to_apply=%add.1 | all-reduce | flops 1744 | bytes 13952
  101.6 34.5 %fusion.3 = (bf16[1024,3072]{1,0:T(8,128)(2,1)S(1)}, f32[1024,3072]{1,0:T(8,128)}) fusion(f32[3072]{0:T(1024)S(1)} %copy-done.61, bf16[768,3072]{1,0:T(8,128)(2,1)S(1)} %bitcast.205, f32[1024,768]{1,0:T(8,128)S(1)} %get-tuple-element.63, f32[768]{0:T(1024)S(1)} %copy-done.37, f32[768]{0:T(1024)S(1)} %copy-done.32, f32[1024]{0:T(1024)S(1)} %add_rsqrt_fusion.1, ...), kind=kOutput, calls=%fused_computation.6 | convolution fusion | flops 5043388416 | bytes 26765312 | tf_op jit(solution)/shard_map/dot_general | solution.py:115
  136.2 5.5 fusion.100
  145.0 68.0 %all_gather.18 = bf16[512,768]{1,0:T(8,128)(2,1)S(1)} all-gather(bf16[16,768]{1,0:T(8,128)(2,1)S(1)} %fusion.71), channel_id=1, replica_groups=mesh['stream'=2,'dp'=16] {'stream','dp'}, dimensions={0}, use_global_device_ids=true | all-gather | bytes 811008 | tf_op jit(solution)/shard_map/all_gather | solution.py:125
  221.3 91.3 %reduce-scatter.4.cloned.1.call-done = f32[16,768]{1,0:T(8,128)} async-done(((f32[512,768]{1,0:T(8,128)}), f32[16,768]{1,0:T(8,128)}) %reduce-scatter.4.cloned.1.call-update) | async-done | bytes 49168 | tf_op jit(solution)/shard_map/reduce_scatter | solution.py:155
  327.4 10.3 fusion.86
  337.7 12.5 convert_reduce_fusion
  350.2 6.5 multiply_reduce_fusion.1
  356.7 8.9 convolution_bitcast_fusion
  374.9 6.4 convert_reduce_fusion.3
  385.9 4.9 fusion.41
  393.0 10.8 reshape.345
  403.8 9.6 copy.134
  460.0 21.2 %dynamic-update-slice.7 = f32[7087104]{0:T(1024)} dynamic-update-slice(f32[7087104]{0:T(1024)} %constant_dynamic-update-slice_fusion.8, f32[589824]{0:T(1024)} %reshape.341, s32[]{} %constant.186) | dynamic-update-slice | bytes 4718596
  481.2 21.2 %dynamic-update-slice.8 = f32[7087104]{0:T(1024)} dynamic-update-slice(f32[7087104]{0:T(1024)} %dynamic-update-slice.7, f32[589824]{0:T(1024)} %reshape.342, s32[]{} %constant.187) | dynamic-update-slice | bytes 4718596
  503.7 20.2 %dynamic-update-slice.10 = f32[7087104]{0:T(1024)} dynamic-update-slice(f32[7087104]{0:T(1024)} %constant_dynamic-update-slice_fusion.7, f32[589824]{0:T(1024)S(1)} %reshape.343, s32[]{} %constant.189) | dynamic-update-slice | bytes 4718596
  527.8 80.6 %dynamic-update-slice.14 = f32[7087104]{0:T(1024)} dynamic-update-slice(f32[7087104]{0:T(1024)} %constant_dynamic-update-slice_fusion.4, f32[2359296]{0:T(1024)} %bitcast.173, s32[]{} %constant.193) | dynamic-update-slice | bytes 18874372
  609.7 80.7 %dynamic-update-slice.16 = f32[7087104]{0:T(1024)} dynamic-update-slice(f32[7087104]{0:T(1024)} %constant_dynamic-update-slice_fusion.3, f32[2359296]{0:T(1024)} %reshape.345, s32[]{} %constant.195) | dynamic-update-slice | bytes 18874372
  694.4 37.8 %reshape.346 = f32[32,221472]{1,0:T(8,128)} reshape(f32[7087104]{0:T(1024)} %constant_dynamic-update-slice_fusion) | data formatting | bytes 56696832 | tf_op jit(solution)/shard_map/reshape | solution.py:240
  732.2 20.9 %pad.6 = f32[32,221568]{1,0:T(8,128)} pad(f32[32,221472]{1,0:T(8,128)} %reshape.346, f32[]{:T(128)} %constant.120.clone.1), padding=0_0x0_96 | pad | bytes 56709124 | tf_op jit(solution)/shard_map/jit(_pad)/pad | solution.py:241
  753.1 25.4 %reshape.347 = f32[55392,128]{1,0:T(8,128)} reshape(f32[32,221568]{1,0:T(8,128)} %pad.6) | data formatting | bytes 56721408 | tf_op jit(solution)/shard_map/reshape | solution.py:241
  778.5 605.0 %fusion = f32[1744,128]{1,0:T(8,128)S(1)} fusion(f32[55392,128]{1,0:T(8,128)} %reshape.347), kind=kCustom, calls=%all-reduce-scatter | all-reduce-scatter fusion | flops 7143425 | bytes 29253632
  1399.2 96.8 %all-gather.4.cloned.1.call-done = bf16[32,1731,128]{2,1,0:T(8,128)(2,1)} async-done(((bf16[1,1731,128]{2,1,0:T(8,128)(2,1)}), bf16[32,1731,128]{2,1,0:T(8,128)(2,1)}) %all-gather.4.cloned.1.call-update) | async-done | bytes 14180368 | tf_op jit(solution)/shard_map/all_gather | solution.py:243
  1496.0 12.8 copy.209
  1508.8 9.7 slice_convert_fusion
  1518.6 36.5 %reshape.367 = f32[7087104]{0:T(1024)} reshape(f32[32,221472]{1,0:T(8,128)} %slice_convert_fusion) | data formatting | bytes 56696832
  1557.8 8.3 slice.115
  1566.1 31.3 %slice.87 = f32[9228,768]{1,0:T(8,128)} reshape(f32[7087104]{0:T(1024)} %reshape.367) | data formatting | bytes 56696832 | tf_op jit(solution)/shard_map/slice | solution.py:251
  1597.4 8.1 slice.117
  1605.5 7.7 fusion.97
  1613.1 11.0 reshape.350
  (263 shorter events, 154.8 us)
Async XLA Ops:
  7.2 89.9 %copy-start = (bf16[768,768]{1,0:T(8,128)(2,1)S(1)}, bf16[768,768]{1,0:T(8,128)(2,1)}, u32[]{:S(2)}) copy-start(bf16[768,768]{1,0:T(8,128)(2,1)} %param.27) | copy-start | bytes 3538948
  7.2 305.4 %reduce-scatter.4.cloned.1.call-start = ((), (), s32[]{:S(2)}) async-start(), calls=%async_computation.1 | async-start | bytes 1622016 | tf_op jit(solution)/shard_map/reduce_scatter | solution.py:155
  69.0 24.6 %copy-start.29 = (pred[128,128]{0,1:T(8,128)(4,1)}, pred[128,128]{0,1:T(8,128)(4,1)S(1)}, u32[]{:S(2)}) copy-start(pred[128,128]{0,1:T(8,128)(4,1)S(1)} %broadcast_compare_fusion) | copy-start | bytes 49156
  97.2 38.9 %slice-start.2 = ((s8[4718592]{0:T(1024)(128)(4,1)}), s8[4194304]{0:T(1024)(128)(4,1)S(1)}, s32[]{:S(2)}) async-start(s8[4718592]{0:T(1024)(128)(4,1)} %bitcast.200), calls=%async_computation.5 | async-start | bytes 8388608
  99.0 37.2 %copy-start.5 = (f32[1024,768]{1,0:T(8,128)}, f32[1024,768]{1,0:T(8,128)S(1)}, u32[]{:S(2)}) copy-start(f32[1024,768]{1,0:T(8,128)S(1)} %get-tuple-element.63) | copy-start | bytes 9437188
  101.6 34.6 %slice-start.3 = ((s8[4718592]{0:T(1024)(128)(4,1)}), s8[524288]{0:T(1024)(128)(4,1)S(1)}, s32[]{:S(2)}) async-start(s8[4718592]{0:T(1024)(128)(4,1)} %bitcast.200), calls=%async_computation.6 | async-start | bytes 1048576
  101.6 34.6 %copy-start.65 = (f32[768]{0:T(1024)S(1)}, f32[768]{0:T(1024)}, u32[]{:S(2)}) copy-start(f32[768]{0:T(1024)} %param.34) | copy-start | bytes 9220
  142.5 70.5 %copy-start.39 = (s32[256]{0:T(256)S(1)}, s32[256]{0:T(256)}, u32[]{:S(2)}) copy-start(s32[256]{0:T(256)} %all-reduce.2) | copy-start | bytes 3076
  142.5 70.5 %copy-start.44 = (s32[16]{0:T(128)S(1)}, s32[16]{0:T(128)}, u32[]{:S(2)}) copy-start(s32[16]{0:T(128)} %param.21) | copy-start | bytes 196
  142.5 70.5 %copy-start.45 = (s32[16]{0:T(128)S(1)}, s32[16]{0:T(128)}, u32[]{:S(2)}) copy-start(s32[16]{0:T(128)} %iota_add_fusion) | copy-start | bytes 196
  142.5 71.1 %copy-start.53 = (f32[16]{0:T(128)S(1)}, f32[16]{0:T(128)}, u32[]{:S(2)}) copy-start(f32[16]{0:T(128)} %select_reduce_fusion.1) | copy-start | bytes 196
  144.3 69.8 %copy-start.18 = (f32[16,1,768]{2,1,0:T(1,128)}, f32[16,1,768]{2,1,0:T(1,128)S(1)}, u32[]{:S(2)}) copy-start(f32[16,1,768]{2,1,0:T(1,128)S(1)} %slice.104) | copy-start | bytes 147460
  145.0 69.2 %copy-start.46 = (f32[16]{0:T(128)}, f32[16]{0:T(128)S(1)}, u32[]{:S(2)}) copy-start(f32[16]{0:T(128)S(1)} %add_rsqrt_fusion.2) | copy-start | bytes 196
  145.0 69.1 %copy-start.31 = (bf16[16,768]{1,0:T(8,128)(2,1)}, bf16[16,768]{1,0:T(8,128)(2,1)S(1)}, u32[]{:S(2)}) copy-start(bf16[16,768]{1,0:T(8,128)(2,1)S(1)} %fusion.71) | copy-start | bytes 73732
  216.7 95.9 %copy-start.19 = (f32[16,1,768]{2,1,0:T(1,128)S(1)}, f32[16,1,768]{2,1,0:T(1,128)}, u32[]{:S(2)}) copy-start(f32[16,1,768]{2,1,0:T(1,128)} %copy-done.18) | copy-start | bytes 147460
  216.7 96.8 %copy-start.52 = (f32[16]{0:T(128)S(1)}, f32[16]{0:T(128)}, u32[]{:S(2)}) copy-start(f32[16]{0:T(128)} %copy-done.51) | copy-start | bytes 196
  216.7 96.8 %copy-start.47 = (f32[16]{0:T(128)S(1)}, f32[16]{0:T(128)}, u32[]{:S(2)}) copy-start(f32[16]{0:T(128)} %copy-done.46) | copy-start | bytes 196
  216.7 101.0 %copy-start.34 = (f32[768]{0:T(1024)S(1)}, f32[768]{0:T(1024)}, u32[]{:S(2)}) copy-start(f32[768]{0:T(1024)} %param.35) | copy-start | bytes 9220
  216.7 101.0 %copy-start.36 = (f32[1024]{0:T(1024)S(1)}, f32[1024]{0:T(1024)}, u32[]{:S(2)}) copy-start(f32[1024]{0:T(1024)} %copy-done.35) | copy-start | bytes 12292
  217.9 1278.2 %all-gather.4.cloned.1.call-start = ((), (), s32[]{:S(2)}) async-start(), calls=%async_computation.2 | async-start | bytes 14665728 | tf_op jit(solution)/shard_map/all_gather | solution.py:243
  323.3 14.4 slice-start.4
  327.4 22.8 %slice-start.8 = ((s8[4718592]{0:T(1024)(128)(4,1)}), s8[4194304]{0:T(1024)(128)(4,1)S(1)}, s32[]{:S(2)}) async-start(s8[4718592]{0:T(1024)(128)(4,1)} %bitcast.206), calls=%async_computation.11 | async-start | bytes 8388608
  337.7 12.5 copy-start.6
  337.7 12.5 slice-start.9
  502.4 22.8 %copy-start.50 = (f32[768]{0:T(1024)S(1)}, f32[768]{0:T(1024)}, u32[]{:S(2)}) copy-start(f32[768]{0:T(1024)} %get-tuple-element.32) | copy-start | bytes 9220
  502.4 24.1 %copy-start.49 = (f32[768]{0:T(1024)S(1)}, f32[768]{0:T(1024)}, u32[]{:S(2)}) copy-start(f32[768]{0:T(1024)} %get-tuple-element.37) | copy-start | bytes 9220
  527.8 80.6 %copy-start.43 = (f32[3072]{0:T(1024)S(1)}, f32[3072]{0:T(1024)}, u32[]{:S(2)}) copy-start(f32[3072]{0:T(1024)} %get-tuple-element.77) | copy-start | bytes 36868
  609.7 80.8 %copy-start.41 = (f32[768]{0:T(1024)S(1)}, f32[768]{0:T(1024)}, u32[]{:S(2)}) copy-start(f32[768]{0:T(1024)} %get-tuple-element.40) | copy-start | bytes 9220
  609.7 82.1 %copy-start.42 = (f32[768]{0:T(1024)S(1)}, f32[768]{0:T(1024)}, u32[]{:S(2)}) copy-start(f32[768]{0:T(1024)} %get-tuple-element.30) | copy-start | bytes 9220
  609.7 83.4 %copy-start.40 = (f32[768]{0:T(1024)S(1)}, f32[768]{0:T(1024)}, u32[]{:S(2)}) copy-start(f32[768]{0:T(1024)} %get-tuple-element.35) | copy-start | bytes 9220
  778.5 611.8 %copy-start.24 = (bf16[8,128,12,64]{1,0,3,2:T(8,128)(2,1)S(1)}, bf16[8,128,12,64]{1,0,3,2:T(8,128)(2,1)}, u32[]{:S(2)}) copy-start(bf16[8,128,12,64]{1,0,3,2:T(8,128)(2,1)} %copy-done.23) | copy-start | bytes 4718596
  1383.6 4.4 collective-permute-start
  (48 other events, 168.0 us)
Sparse Core Ops, SparseCore 0:
  218.0 94.5 reduce-scatter.3
  1390.4 105.5 all-gather.3
